TPU v7x, 512 devices: a whole 4x8x8 slice. The times are simulated.
512 devices in a mesh: band: 8 (over y), gy: 8 (over z), gz: 8 (over x, core).
Axes of the slice: x: 4, y: 8, z: 8, core: 2. Of those that a mesh axis runs over, the one named last changes fastest.
Arguments:
- orbitals: float32 [1024, 48, 3840], P('band', 'gy', 'gz'), may hold values from -6 to 6
- occupied: bfloat16 [1024, 48, 3840], P('band', 'gy', 'gz'), may hold values from -6 to 6
- eigen: float32 [1024], P('band'), may hold values from -1.5 to 0
- potential: float32 [48, 3840], P('gy', 'gz'), may hold values from -2 to 0.5
- perturbation: float32 [48, 3840], P('gy', 'gz'), may hold values from 0.2 to 1.5
- precondition: float32 [48, 3840], P('gy', 'gz'), may hold values from 0.05 to 0.3
Outputs:
- updated: float32 [1024, 48, 3840], P('band', 'gy', 'gz')
- resid_norm: float32 [1024], P('band')
All inputs are finite; a program needn't handle non-finite values.
Results may differ from a plain program's by a relative error of at most 0.0008.
Values may be sent and summed in bfloat16 or wider, within the bound.
A program may use at most 128 MiB of HBM per device.

v0:
```python
import jax
import jax.numpy as jnp
from jax import lax
from jax.sharding import PartitionSpec as P

NX = 80
stencil = (-205.0 / 72.0, 8.0 / 5.0, -1.0 / 5.0, 8.0 / 315.0, -1.0 / 560.0)


def extended(block, sides, width):
    for axis, dim in sides:
        count = lax.axis_size(axis)
        forward = [(i, i + 1) for i in range(count - 1)]
        forward.append((count - 1, 0))
        backward = [(target, source) for source, target in forward]
        low = lax.ppermute(
            lax.slice_in_dim(block, block.shape[dim] - width, None, axis=dim), axis, forward
        )
        high = lax.ppermute(lax.slice_in_dim(block, 0, width, axis=dim), axis, backward)
        block = jnp.concatenate([low, block, high], axis=dim)
    return block


def along_x(field, dist):
    flat = field.shape[-1]
    position = lax.broadcasted_iota(jnp.int32, (flat,), 0) % NX
    lower = jnp.where(position >= dist, jnp.roll(field, dist, -1), jnp.roll(field, dist - NX, -1))
    upper = jnp.where(
        position < NX - dist, jnp.roll(field, -dist, -1), jnp.roll(field, NX - dist, -1)
    )
    return lower + upper


def laplace(field):
    rows_y = field.shape[1]
    flat = field.shape[2]
    padded_y = extended(field, (("gy", 1),), 4)
    padded_z = extended(field, (("gz", 2),), 4 * NX)
    total = 3.0 * stencil[0] * field
    for dist in range(1, 5):
        pair_y = (
            padded_y[:, 4 + dist : 4 + dist + rows_y, :]
            + padded_y[:, 4 - dist : 4 - dist + rows_y, :]
        )
        pair_z = (
            padded_z[:, :, (4 + dist) * NX : (4 + dist) * NX + flat]
            + padded_z[:, :, (4 - dist) * NX : (4 - dist) * NX + flat]
        )
        total = total + stencil[dist] * (along_x(field, dist) + pair_y + pair_z)
    return total


def on_device(orbitals, occupied, eigen, potential, perturbation, precondition):
    band_rows, rows_y, flat = orbitals.shape
    cells = NX * rows_y * lax.axis_size("gy") * (flat // NX) * lax.axis_size("gz")
    occ_wide = occupied.astype(jnp.float32)
    resid = (
        -0.5 * laplace(orbitals)
        + (potential[None] - eigen[:, None, None]) * orbitals
        + perturbation[None] * occ_wide
    )
    squares = jnp.sum(resid * resid, axis=(1, 2))
    squares = lax.psum(squares, ("gy", "gz"))
    trial = orbitals - precondition[None] * resid
    trial_low = trial.astype(jnp.bfloat16)
    partial_margins = jnp.einsum(
        "oyc,ryc->or",
        lax.all_gather(occupied, "band", axis=0, tiled=True),
        trial_low,
        preferred_element_type=jnp.float32,
    )
    margins = lax.psum(partial_margins, ("gy", "gz"))
    norms = jnp.sqrt(squares / cells + 1e-06)
    coeff = (margins / cells).astype(jnp.bfloat16)
    correction = jnp.einsum(
        "or,oyc->ryc",
        coeff,
        lax.all_gather(occupied, "band", axis=0, tiled=True),
        preferred_element_type=jnp.float32,
    )
    updated = trial - correction
    return (updated, norms)


def solution(mesh):
    placed = (
        P("band", "gy", "gz"),
        P("band", "gy", "gz"),
        P("band"),
        P("gy", "gz"),
        P("gy", "gz"),
        P("gy", "gz"),
    )
    return jax.shard_map(
        on_device,
        mesh=mesh,
        in_specs=placed,
        out_specs=(P("band", "gy", "gz"), P("band")),
        check_vma=False,
    )
```

profile of v0, /device:TPU:8, one launch (start us, length us, event | category | flops | bytes accessed | tf_op | source)
XLA Modules:
  0.0 306.1 jit_solution(4770405374905059568)
XLA Ops:
  7.2 0.7 all-gather.2.cloned.1.call-update
  8.0 1.7 fusion.56
  9.7 4.3 %collective-permute-start.1 = (f32[128,4,480]{0,2,1:T(8,128)S(1)}, f32[128,4,480]{0,2,1:T(8,128)S(1)}, u32[]{:S(2)}, u32[]{:S(2)}) collective-permute-start(f32[128,4,480]{0,2,1:T(8,128)S(1)} %get-tuple-element.37), channel_id=1, source_target_pairs={{0,8},{8,16},{16,24},{24,32},{32,40},{40,48},{48,56},{56,0},{1,9},... | collective-permute-start | bytes 2949128 | tf_op jit(solution)/shard_map/ppermute | solution.py:16
  14.2 8.6 %collective-permute-start = (f32[128,4,480]{0,2,1:T(8,128)S(1)}, f32[128,4,480]{0,2,1:T(8,128)S(1)}, u32[]{:S(2)}, u32[]{:S(2)}) collective-permute-start(f32[128,4,480]{0,2,1:T(8,128)S(1)} %get-tuple-element.36), channel_id=1, source_target_pairs={{8,0},{16,8},{24,16},{32,24},{40,32},{48,40},{56,48},{0,56},{9,1},... | collective-permute-start | bytes 2949128 | tf_op jit(solution)/shard_map/ppermute | solution.py:19
  22.8 2.7 collective-permute-start.2
  26.1 0.8 fusion.47
  27.0 0.8 fusion.51
  27.8 0.9 fusion.55
  28.7 1.2 fusion.46
  29.9 1.6 fusion.50
  31.5 1.9 fusion.45
  33.4 1.9 fusion.49
  35.3 1.8 fusion.53
  37.1 1.8 fusion.41
  40.0 1.6 fusion.54
  42.7 1.6 fusion.42
  44.5 0.6 constant_dynamic-update-slice_fusion.1
  45.4 0.6 copy-done.2
  46.0 13.7 %multiply_reduce_fusion = (f32[128]{0:T(128)}, f32[128,6,480]{0,2,1:T(8,128)S(1)}) fusion(bf16[128,6,480]{0,2,1:T(8,128)(2,1)} %param.7, f32[6,480]{1,0:T(8,128)S(1)} %copy-done.2, f32[128,6,480]{0,2,1:T(8,128)S(1)} %copy-done, f32[128]{0:T(128)} %param.8, f32[6,480]{1,0:T(8,128)S(1)} %copy-done.3, f32[128,6,800]{0,2,1:T(8,128)S(1)} %get-tuple-element.39, ...), kind=kLoop, calls=%fused_computation.39 | loop fusion | flops 22855552 | bytes 50900224 | tf_op jit(solution)/shard_map/reduce_sum | solution.py:62
  59.7 35.2 %all-gather.2.cloned.1.call-done = bf16[1024,6,480]{0,2,1:T(8,128)(2,1)} async-done(((bf16[128,6,480]{0,2,1:T(8,128)(2,1)}), bf16[1024,6,480]{0,2,1:T(8,128)(2,1)}) %all-gather.2.cloned.1.call-update) | async-done | bytes 5898256 | tf_op jit(solution)/shard_map/all_gather | solution.py:68
  94.9 6.2 %convolution_bitcast_fusion = f32[1024,128]{1,0:T(8,128)} fusion(bf16[1024,6,480]{0,2,1:T(8,128)(2,1)} %all-gather.2.cloned.1.call-done, f32[128,6,480]{0,2,1:T(8,128)S(1)} %copy-done, f32[128,6,480]{0,2,1:T(8,128)S(1)} %get-tuple-element.3, f32[6,480]{1,0:T(8,128)S(1)} %copy-done.1), kind=kOutput, calls=%fused_computation.42 | convolution fusion | flops 756080640 | bytes 9383168 | tf_op jit(solution)/shard_map/oyc,ryc->or/dot_general | solution.py:66
  101.1 125.7 %psum.15 = f32[128]{0:T(128)S(1)} all-reduce(f32[128]{0:T(128)S(1)} %copy-done.4), channel_id=1, replica_groups=mesh['band'=8,'gy'=8,'gz'=8] {'gy','gz'}, use_global_device_ids=true, to_apply=%region_2.3 | all-reduce | flops 128 | bytes 1024 | tf_op jit(solution)/shard_map/psum | solution.py:63
  227.3 66.2 %all-reduce.2.cloned.1.call-done = f32[1024,128]{1,0:T(8,128)} async-done(((f32[1024,128]{1,0:T(8,128)}), f32[1024,128]{1,0:T(8,128)}) %all-reduce.2.cloned.1.call-update) | async-done | bytes 524304 | tf_op jit(solution)/shard_map/psum | solution.py:72
  293.6 5.7 %convolution_subtract_fusion = f32[128,6,480]{0,2,1:T(8,128)} fusion(bf16[1024,6,480]{0,2,1:T(8,128)(2,1)} %all-gather.2.cloned.1.call-done, f32[128,6,480]{0,2,1:T(8,128)S(1)} %copy-done, f32[128,6,480]{0,2,1:T(8,128)S(1)} %get-tuple-element.3, f32[6,480]{1,0:T(8,128)S(1)} %copy-done.1, f32[1024,128]{1,0:T(8,128)} %all-reduce.2.cloned.1.call-done), kind=kOutput, calls=%fused_computation.41 | convolution fusion | flops 756342784 | bytes 10857728 | tf_op jit(solution)/shard_map/or,oyc->ryc/dot_general | solution.py:75
  (32 shorter events, 4.0 us)
Async XLA Ops:
  7.2 87.7 %all-gather.2.cloned.1.call-start = ((), (), s32[]{:S(2)}) async-start(), calls=%async_computation | async-start | bytes 6635520 | tf_op jit(solution)/shard_map/all_gather | solution.py:68
  7.9 6.1 %copy-start = (f32[128,6,480]{0,2,1:T(8,128)S(1)}, f32[128,6,480]{0,2,1:T(8,128)}, u32[]{:S(2)}) copy-start(f32[128,6,480]{0,2,1:T(8,128)} %param.6) | copy-start | bytes 4423684
  7.9 285.7 %all-reduce.2.cloned.1.call-start = ((), (), s32[]{:S(2)}) async-start(), calls=%async_computation.1 | async-start | bytes 1048576 | tf_op jit(solution)/shard_map/psum | solution.py:72
  9.7 34.7 %collective-permute-start.1 = (f32[128,4,480]{0,2,1:T(8,128)S(1)}, f32[128,4,480]{0,2,1:T(8,128)S(1)}, u32[]{:S(2)}, u32[]{:S(2)}) collective-permute-start(f32[128,4,480]{0,2,1:T(8,128)S(1)} %get-tuple-element.37), channel_id=1, source_target_pairs={{0,8},{8,16},{16,24},{24,32},{32,40},{40,48},{48,56},{56,0},{1,9},... | collective-permute-start | bytes 2949128 | tf_op jit(solution)/shard_map/ppermute | solution.py:16
  14.2 30.3 %collective-permute-start.3 = (f32[128,6,320]{0,2,1:T(8,128)S(1)}, f32[128,6,320]{0,2,1:T(8,128)S(1)}, u32[]{:S(2)}, u32[]{:S(2)}) collective-permute-start(f32[128,6,320]{0,2,1:T(8,128)S(1)} %get-tuple-element.43), channel_id=1, source_target_pairs={{0,1},{1,2},{2,3},{3,4},{4,5},{5,6},{6,7},{7,0},{8,9},{9,10},{10,1... | collective-permute-start | bytes 2949128 | tf_op jit(solution)/shard_map/ppermute | solution.py:16
  14.2 31.0 %collective-permute-start = (f32[128,4,480]{0,2,1:T(8,128)S(1)}, f32[128,4,480]{0,2,1:T(8,128)S(1)}, u32[]{:S(2)}, u32[]{:S(2)}) collective-permute-start(f32[128,4,480]{0,2,1:T(8,128)S(1)} %get-tuple-element.36), channel_id=1, source_target_pairs={{8,0},{16,8},{24,16},{32,24},{40,32},{48,40},{56,48},{0,56},{9,1},... | collective-permute-start | bytes 2949128 | tf_op jit(solution)/shard_map/ppermute | solution.py:19
  22.8 22.5 %collective-permute-start.2 = (f32[128,6,320]{0,2,1:T(8,128)S(1)}, f32[128,6,320]{0,2,1:T(8,128)S(1)}, u32[]{:S(2)}, u32[]{:S(2)}) collective-permute-start(f32[128,6,320]{0,2,1:T(8,128)S(1)} %get-tuple-element.42), channel_id=1, source_target_pairs={{1,0},{2,1},{3,2},{4,3},{5,4},{6,5},{7,6},{0,7},{9,8},{10,9},{11,1... | collective-permute-start | bytes 2949128 | tf_op jit(solution)/shard_map/ppermute | solution.py:19
  45.2 0.7 copy-start.2
  45.3 0.7 copy-start.3
  46.0 48.9 %copy-start.1 = (f32[6,480]{1,0:T(8,128)S(1)}, f32[6,480]{1,0:T(8,128)}, u32[]{:S(2)}) copy-start(f32[6,480]{1,0:T(8,128)} %param.11) | copy-start | bytes 34564
  94.9 6.3 %copy-start.4 = (f32[128]{0:T(128)S(1)}, f32[128]{0:T(128)}, u32[]{:S(2)}) copy-start(f32[128]{0:T(128)} %get-tuple-element.2) | copy-start | bytes 1540
Sparse Core Ops, SparseCore 0:
  10.0 84.8 all-gather.1
  101.2 192.2 all-reduce.1
where the time goes:
time: 306 us
  blocking collectives  126 us (41%)
  waiting for transfers between devices  102 us (33%)
  local copies, waits for them, and re-layouts  20.1 us (7%)
  other arithmetic  16.5 us (5%)
  starting transfers between devices  15.6 us (5%)
  between operations  14.2 us (5%)
  matrix products  11.9 us (4%)
    psum x1, blocking collectives, on_device(): squares = lax.psum(squares, ('gy', 'gz'))  126 us
    psum x1, waiting for transfers between devices, on_device(): margins = lax.psum(partial_margins, ('gy', 'gz'))  66.2 us
    all_gather x1, waiting for transfers between devices, on_device(): lax.all_gather(occupied, 'band', axis=0, tiled=True)  35.2 us
    reduce_sum x1, other arithmetic, on_device(): squares = jnp.sum(resid * resid, axis=(1, 2))  13.7 us
    ppermute x2, starting transfers between devices, extended(): lax.ppermute(lax.slice_in_dim(block, 0, width, axis=dim), axis, backward)  11.2 us
    slice x8, local copies, waits for them, and re-layouts, along_x(): jnp.roll(field, dist - NX, -1)  8.63 us
    slice x8, local copies, waits for them, and re-layouts, along_x(): jnp.roll(field, dist, -1)  8.03 us
    dot_general x1, matrix products, on_device(): jnp.einsum('oyc,ryc->or', lax.all_gather(occupied, 'band', axis=0, tiled=...  6.24 us
  transfers between devices with their start and end apart: 6, of which 2 were waited for; matrix products, arithmetic and copies ran while one was open for 12% of the time, Pallas kernels for 0%

commit v1 on v0

--- a/solution.py
+++ b/solution.py
@@ -5,6 +5,30 @@
 
 NX = 80
 stencil = (-205.0 / 72.0, 8.0 / 5.0, -1.0 / 5.0, 8.0 / 315.0, -1.0 / 560.0)
+
+
+def work_both_ways(x, axis, dim, work, out_dim):
+    count, index, span = (lax.axis_size(axis), lax.axis_index(axis), x.shape[dim])
+    right = [(i, (i + 1) % count) for i in range(count)]
+    behind = [(b, a) for a, b in right]
+    lower, upper = (lax.ppermute(x, axis, right), lax.ppermute(x, axis, behind))
+    made = work(x, index * span)
+    length = made.shape[out_dim]
+    out = jnp.zeros((*made.shape[:out_dim], count * length, *made.shape[out_dim + 1 :]), made.dtype)
+
+    def put(out, made, source):
+        return lax.dynamic_update_slice_in_dim(out, made, source * length, axis=out_dim)
+
+    out = put(out, made, index)
+    for step in range(1, count // 2 + 1):
+        below, above = ((index - step) % count, (index + step) % count)
+        held = (lower, upper)
+        if step < count // 2:
+            lower, upper = (lax.ppermute(lower, axis, right), lax.ppermute(upper, axis, behind))
+        out = put(out, work(held[0], below * span), below)
+        if 2 * step < count:
+            out = put(out, work(held[1], above * span), above)
+    return out
 
 
 def extended(block, sides, width):
@@ -63,11 +87,14 @@
     squares = lax.psum(squares, ("gy", "gz"))
     trial = orbitals - precondition[None] * resid
     trial_low = trial.astype(jnp.bfloat16)
-    partial_margins = jnp.einsum(
-        "oyc,ryc->or",
-        lax.all_gather(occupied, "band", axis=0, tiled=True),
-        trial_low,
-        preferred_element_type=jnp.float32,
+    partial_margins = work_both_ways(
+        occupied,
+        "band",
+        0,
+        lambda shard, at: jnp.einsum(
+            "oyc,ryc->or", shard, trial_low, preferred_element_type=jnp.float32
+        ),
+        0,
     )
     margins = lax.psum(partial_margins, ("gy", "gz"))
     norms = jnp.sqrt(squares / cells + 1e-06)

time: 306 us -> 329 us (1.075)
  starting transfers between devices: 15.6 us -> 37.6 us
  waiting for transfers between devices: 102 us -> 93.7 us
  local copies, waits for them, and re-layouts: 20.1 us -> 24.9 us
    all_gather x1, waiting for transfers between devices: 35.2 us -> 0.01 us  [on_device(): lax.all_gather(occupied, 'band', axis=0, tiled=True)]
    ppermute x0 -> x7, starting transfers between devices: none -> 25.8 us  [the longest x3 10.5 us: work_both_ways(): lax.ppermute(lower, axis, right)]
    ppermute x0 -> x7, waiting for transfers between devices: none -> 24.5 us  [the longest x3 23 us: work_both_ways(): lax.ppermute(lower, axis, right)]
    dot_general x1 -> x8, matrix products: 6.24 us -> 8 us  [on_device(): jnp.einsum('oyc,ryc->or', shard, trial_low, preferred_element_type=jnp.fl...]
  transfers between devices with their start and end apart: 6 -> 13, of which waited for: 2 -> 5; matrix products, arithmetic and copies ran while one was open for 12% -> 14% of each run, Pallas kernels for 0% -> 0%
where the time goes in v1:
time: 329 us
  blocking collectives  129 us (39%)
  waiting for transfers between devices  93.7 us (28%)
  starting transfers between devices  37.6 us (11%)
  local copies, waits for them, and re-layouts  24.9 us (8%)
  between operations  16 us (5%)
  other arithmetic  14.3 us (4%)
  matrix products  13.7 us (4%)
    psum x1, blocking collectives, on_device(): squares = lax.psum(squares, ('gy', 'gz'))  129 us
    psum x1, waiting for transfers between devices, on_device(): margins = lax.psum(partial_margins, ('gy', 'gz'))  67.5 us
    ppermute x3, waiting for transfers between devices, work_both_ways(): lax.ppermute(lower, axis, right)  23 us
    reduce_sum x1, other arithmetic, on_device(): squares = jnp.sum(resid * resid, axis=(1, 2))  13.3 us
    ppermute x3, starting transfers between devices, work_both_ways(): lax.ppermute(lower, axis, right)  10.5 us
    ppermute x2, starting transfers between devices, extended(): lax.ppermute(lax.slice_in_dim(block, 0, width, axis=dim), axis, backward)  9.81 us
    ppermute x2, starting transfers between devices, work_both_ways(): lower, upper = (lax.ppermute(x, axis, right), lax.ppermute(x, axis, behind))  9.79 us
    slice x8, local copies, waits for them, and re-layouts, along_x(): jnp.roll(field, dist - NX, -1)  8.95 us
  transfers between devices with their start and end apart: 13, of which 5 were waited for; matrix products, arithmetic and copies ran while one was open for 14% of the time, Pallas kernels for 0%

profile of v1, /device:TPU:8, one launch (start us, length us, event | category | flops | bytes accessed | tf_op | source)
XLA Modules:
  0.0 328.7 jit_solution(14691329094101569301)
XLA Ops:
  8.1 3.6 %collective-permute-start.4 = (bf16[128,6,480]{0,2,1:T(8,128)(2,1)}, bf16[128,6,480]{0,2,1:T(8,128)(2,1)}, u32[]{:S(2)}, u32[]{:S(2)}) collective-permute-start(bf16[128,6,480]{0,2,1:T(8,128)(2,1)} %param.7), channel_id=1, source_target_pairs={{0,64},{64,128},{128,192},{192,256},{256,320},{320,384},{384,448},... | collective-permute-start | bytes 2211848 | tf_op jit(solution)/shard_map/ppermute | solution.py:14
  11.7 6.2 %collective-permute-start.5 = (bf16[128,6,480]{0,2,1:T(8,128)(2,1)}, bf16[128,6,480]{0,2,1:T(8,128)(2,1)}, u32[]{:S(2)}, u32[]{:S(2)}) collective-permute-start(bf16[128,6,480]{0,2,1:T(8,128)(2,1)} %param.7), channel_id=1, source_target_pairs={{64,0},{128,64},{192,128},{256,192},{320,256},{384,320},{448,384},... | collective-permute-start | bytes 2211848 | tf_op jit(solution)/shard_map/ppermute | solution.py:14
  17.9 3.0 fusion.64
  20.8 1.9 collective-permute-start.1
  24.2 7.1 %collective-permute-start = (f32[128,4,480]{0,2,1:T(8,128)}, f32[128,4,480]{0,2,1:T(8,128)S(1)}, u32[]{:S(2)}, u32[]{:S(2)}) collective-permute-start(f32[128,4,480]{0,2,1:T(8,128)} %get-tuple-element.36), channel_id=1, source_target_pairs={{8,0},{16,8},{24,16},{32,24},{40,32},{48,40},{56,48},{0,56},{9,1},... | collective-permute-start | bytes 2949128 | tf_op jit(solution)/shard_map/ppermute | solution.py:43
  31.4 1.8 fusion.53
  33.2 1.8 fusion.57
  35.0 1.8 fusion.61
  36.8 1.9 fusion.49
  38.7 1.6 fusion.54
  40.3 1.6 fusion.58
  41.9 1.7 fusion.62
  46.3 2.7 collective-permute-start.2
  50.6 3.5 %collective-permute-start.6 = (bf16[128,6,480]{0,2,1:T(8,128)(2,1)}, bf16[128,6,480]{0,2,1:T(8,128)(2,1)}, u32[]{:S(2)}, u32[]{:S(2)}) collective-permute-start(bf16[128,6,480]{0,2,1:T(8,128)(2,1)} %collective-permute-done.4), channel_id=1, source_target_pairs={{0,64},{64,128},{128,192},{192,256},{256,320},{320,384},{384,448},... | collective-permute-start | bytes 2211848 | tf_op jit(solution)/shard_map/ppermute | solution.py:27
  54.1 2.4 collective-permute-start.7
  61.1 13.3 %multiply_reduce_fusion = (f32[128]{0:T(128)}, f32[128,6,480]{0,2,1:T(8,128)S(1)}) fusion(bf16[128,6,480]{0,2,1:T(8,128)(2,1)S(1)} %copy-done.1, f32[6,480]{1,0:T(8,128)S(1)} %copy-done.6, f32[128,6,480]{0,2,1:T(8,128)S(1)} %copy-done, f32[128]{0:T(128)S(1)} %copy-done.8, f32[6,480]{1,0:T(8,128)S(1)} %copy-done.7, f32[128,6,800]{0,2,1:T(8,128)S(1)} %get-tuple-element.39, ...), kind=kLoop, calls=%fused_computation.39 | loop fusion | flops 22855552 | bytes 50900224 | tf_op jit(solution)/shard_map/reduce_sum | solution.py:86
  75.3 3.7 %collective-permute-start.8 = (bf16[128,6,480]{0,2,1:T(8,128)(2,1)}, bf16[128,6,480]{0,2,1:T(8,128)(2,1)S(1)}, u32[]{:S(2)}, u32[]{:S(2)}) collective-permute-start(bf16[128,6,480]{0,2,1:T(8,128)(2,1)} %collective-permute-done.6), channel_id=1, source_target_pairs={{0,64},{64,128},{128,192},{192,256},{256,320},{320,384},{384,448},... | collective-permute-start | bytes 2211848 | tf_op jit(solution)/shard_map/ppermute | solution.py:27
  82.2 3.1 collective-permute-start.9
  86.9 9.9 %collective-permute-done.8 = bf16[128,6,480]{0,2,1:T(8,128)(2,1)S(1)} collective-permute-done((bf16[128,6,480]{0,2,1:T(8,128)(2,1)}, bf16[128,6,480]{0,2,1:T(8,128)(2,1)S(1)}, u32[]{:S(2)}, u32[]{:S(2)}) %collective-permute-start.8) | collective-permute-done | bytes 737312 | tf_op jit(solution)/shard_map/ppermute | solution.py:27
  96.8 3.3 %collective-permute-start.10 = (bf16[128,6,480]{0,2,1:T(8,128)(2,1)S(1)}, bf16[128,6,480]{0,2,1:T(8,128)(2,1)S(1)}, u32[]{:S(2)}, u32[]{:S(2)}) collective-permute-start(bf16[128,6,480]{0,2,1:T(8,128)(2,1)S(1)} %collective-permute-done.8), channel_id=1, source_target_pairs={{0,64},{64,128},{128,192},{192,256},{256,320},{320,384},{384,448},... | collective-permute-start | bytes 2211848 | tf_op jit(solution)/shard_map/ppermute | solution.py:27
  104.1 13.1 %collective-permute-done.10 = bf16[128,6,480]{0,2,1:T(8,128)(2,1)S(1)} collective-permute-done((bf16[128,6,480]{0,2,1:T(8,128)(2,1)S(1)}, bf16[128,6,480]{0,2,1:T(8,128)(2,1)S(1)}, u32[]{:S(2)}, u32[]{:S(2)}) %collective-permute-start.10) | collective-permute-done | bytes 737312 | tf_op jit(solution)/shard_map/ppermute | solution.py:27
  119.0 128.6 %psum.15 = f32[128]{0:T(128)S(1)} all-reduce(f32[128]{0:T(128)S(1)} %copy-done.9), channel_id=1, replica_groups=mesh['band'=8,'gy'=8,'gz'=8] {'gy','gz'}, use_global_device_ids=true, to_apply=%region_2.3 | all-reduce | flops 128 | bytes 1024 | tf_op jit(solution)/shard_map/psum | solution.py:87
  248.1 67.5 %all-reduce.2.cloned.1.call-done = f32[1024,128]{1,0:T(8,128)} async-done(((f32[1024,128]{1,0:T(8,128)}), f32[1024,128]{1,0:T(8,128)}) %all-reduce.2.cloned.1.call-update) | async-done | bytes 524304 | tf_op jit(solution)/shard_map/psum | solution.py:99
  315.6 5.7 %convolution_subtract_fusion = f32[128,6,480]{0,2,1:T(8,128)} fusion(bf16[1024,6,480]{0,2,1:T(8,128)(2,1)} %all-gather.2.cloned.1.call-done, f32[128,6,480]{0,2,1:T(8,128)S(1)} %copy-done, f32[128,6,480]{0,2,1:T(8,128)S(1)} %get-tuple-element.3, f32[6,480]{1,0:T(8,128)S(1)} %copy-done.5, f32[1024,128]{1,0:T(8,128)} %all-reduce.2.cloned.1.call-done), kind=kOutput, calls=%fused_computation.41 | convolution fusion | flops 756342784 | bytes 10857728 | tf_op jit(solution)/shard_map/or,oyc->ryc/dot_general | solution.py:102
  (65 shorter events, 22.1 us)
Async XLA Ops:
  8.0 14.7 %copy-start = (f32[128,6,480]{0,2,1:T(8,128)S(1)}, f32[128,6,480]{0,2,1:T(8,128)}, u32[]{:S(2)}) copy-start(f32[128,6,480]{0,2,1:T(8,128)} %param.6) | copy-start | bytes 4423684
  8.0 307.6 %all-reduce.2.cloned.1.call-start = ((), (), s32[]{:S(2)}) async-start(), calls=%async_computation | async-start | bytes 1048576 | tf_op jit(solution)/shard_map/psum | solution.py:99
  8.1 38.3 %collective-permute-start.4 = (bf16[128,6,480]{0,2,1:T(8,128)(2,1)}, bf16[128,6,480]{0,2,1:T(8,128)(2,1)}, u32[]{:S(2)}, u32[]{:S(2)}) collective-permute-start(bf16[128,6,480]{0,2,1:T(8,128)(2,1)} %param.7), channel_id=1, source_target_pairs={{0,64},{64,128},{128,192},{192,256},{256,320},{320,384},{384,448},... | collective-permute-start | bytes 2211848 | tf_op jit(solution)/shard_map/ppermute | solution.py:14
  11.7 38.9 %collective-permute-start.5 = (bf16[128,6,480]{0,2,1:T(8,128)(2,1)}, bf16[128,6,480]{0,2,1:T(8,128)(2,1)}, u32[]{:S(2)}, u32[]{:S(2)}) collective-permute-start(bf16[128,6,480]{0,2,1:T(8,128)(2,1)} %param.7), channel_id=1, source_target_pairs={{64,0},{128,64},{192,128},{256,192},{320,256},{384,320},{448,384},... | collective-permute-start | bytes 2211848 | tf_op jit(solution)/shard_map/ppermute | solution.py:14
  20.8 33.3 %collective-permute-start.1 = (f32[128,4,480]{0,2,1:T(8,128)}, f32[128,4,480]{0,2,1:T(8,128)}, u32[]{:S(2)}, u32[]{:S(2)}) collective-permute-start(f32[128,4,480]{0,2,1:T(8,128)} %get-tuple-element.37), channel_id=1, source_target_pairs={{0,8},{8,16},{16,24},{24,32},{32,40},{40,48},{48,56},{56,0},{1,9},... | collective-permute-start | bytes 2949128 | tf_op jit(solution)/shard_map/ppermute | solution.py:40
  24.2 33.5 %collective-permute-start.3 = (f32[128,6,320]{0,2,1:T(8,128)}, f32[128,6,320]{0,2,1:T(8,128)}, u32[]{:S(2)}, u32[]{:S(2)}) collective-permute-start(f32[128,6,320]{0,2,1:T(8,128)} %get-tuple-element.43), channel_id=1, source_target_pairs={{0,1},{1,2},{2,3},{3,4},{4,5},{5,6},{6,7},{7,0},{8,9},{9,10},{10,1... | collective-permute-start | bytes 2949128 | tf_op jit(solution)/shard_map/ppermute | solution.py:40
  24.2 35.4 %collective-permute-start = (f32[128,4,480]{0,2,1:T(8,128)}, f32[128,4,480]{0,2,1:T(8,128)S(1)}, u32[]{:S(2)}, u32[]{:S(2)}) collective-permute-start(f32[128,4,480]{0,2,1:T(8,128)} %get-tuple-element.36), channel_id=1, source_target_pairs={{8,0},{16,8},{24,16},{32,24},{40,32},{48,40},{56,48},{0,56},{9,1},... | collective-permute-start | bytes 2949128 | tf_op jit(solution)/shard_map/ppermute | solution.py:43
  46.3 14.6 %collective-permute-start.2 = (f32[128,6,320]{0,2,1:T(8,128)}, f32[128,6,320]{0,2,1:T(8,128)S(1)}, u32[]{:S(2)}, u32[]{:S(2)}) collective-permute-start(f32[128,6,320]{0,2,1:T(8,128)} %get-tuple-element.42), channel_id=1, source_target_pairs={{1,0},{2,1},{3,2},{4,3},{5,4},{6,5},{7,6},{0,7},{9,8},{10,9},{11,1... | collective-permute-start | bytes 2949128 | tf_op jit(solution)/shard_map/ppermute | solution.py:43
  50.6 24.7 %collective-permute-start.6 = (bf16[128,6,480]{0,2,1:T(8,128)(2,1)}, bf16[128,6,480]{0,2,1:T(8,128)(2,1)}, u32[]{:S(2)}, u32[]{:S(2)}) collective-permute-start(bf16[128,6,480]{0,2,1:T(8,128)(2,1)} %collective-permute-done.4), channel_id=1, source_target_pairs={{0,64},{64,128},{128,192},{192,256},{256,320},{320,384},{384,448},... | collective-permute-start | bytes 2211848 | tf_op jit(solution)/shard_map/ppermute | solution.py:27
  54.1 28.1 %collective-permute-start.7 = (bf16[128,6,480]{0,2,1:T(8,128)(2,1)}, bf16[128,6,480]{0,2,1:T(8,128)(2,1)}, u32[]{:S(2)}, u32[]{:S(2)}) collective-permute-start(bf16[128,6,480]{0,2,1:T(8,128)(2,1)} %collective-permute-done.5), channel_id=1, source_target_pairs={{64,0},{128,64},{192,128},{256,192},{320,256},{384,320},{448,384},... | collective-permute-start | bytes 2211848 | tf_op jit(solution)/shard_map/ppermute | solution.py:27
  59.7 1.3 copy-start.1
  59.7 1.3 copy-start.3
  59.7 1.3 copy-start.4
  59.7 1.3 copy-start.6
  59.8 1.3 copy-start.7
  59.8 1.3 copy-start.8
  61.1 13.3 %copy-start.5 = (f32[6,480]{1,0:T(8,128)S(1)}, f32[6,480]{1,0:T(8,128)}, u32[]{:S(2)}) copy-start(f32[6,480]{1,0:T(8,128)} %param.11) | copy-start | bytes 34564
  75.3 21.5 %collective-permute-start.8 = (bf16[128,6,480]{0,2,1:T(8,128)(2,1)}, bf16[128,6,480]{0,2,1:T(8,128)(2,1)S(1)}, u32[]{:S(2)}, u32[]{:S(2)}) collective-permute-start(bf16[128,6,480]{0,2,1:T(8,128)(2,1)} %collective-permute-done.6), channel_id=1, source_target_pairs={{0,64},{64,128},{128,192},{192,256},{256,320},{320,384},{384,448},... | collective-permute-start | bytes 2211848 | tf_op jit(solution)/shard_map/ppermute | solution.py:27
  82.2 21.5 %collective-permute-start.9 = (bf16[128,6,480]{0,2,1:T(8,128)(2,1)}, bf16[128,6,480]{0,2,1:T(8,128)(2,1)S(1)}, u32[]{:S(2)}, u32[]{:S(2)}) collective-permute-start(bf16[128,6,480]{0,2,1:T(8,128)(2,1)} %collective-permute-done.7), channel_id=1, source_target_pairs={{64,0},{128,64},{192,128},{256,192},{320,256},{384,320},{448,384},... | collective-permute-start | bytes 2211848 | tf_op jit(solution)/shard_map/ppermute | solution.py:27
  96.8 20.3 %collective-permute-start.10 = (bf16[128,6,480]{0,2,1:T(8,128)(2,1)S(1)}, bf16[128,6,480]{0,2,1:T(8,128)(2,1)S(1)}, u32[]{:S(2)}, u32[]{:S(2)}) collective-permute-start(bf16[128,6,480]{0,2,1:T(8,128)(2,1)S(1)} %collective-permute-done.8), channel_id=1, source_target_pairs={{0,64},{64,128},{128,192},{192,256},{256,320},{320,384},{384,448},... | collective-permute-start | bytes 2211848 | tf_op jit(solution)/shard_map/ppermute | solution.py:27
  104.1 14.9 %copy-start.9 = (f32[128]{0:T(128)S(1)}, f32[128]{0:T(128)}, u32[]{:S(2)}) copy-start(f32[128]{0:T(128)} %get-tuple-element.2) | copy-start | bytes 1540
  117.6 0.8 copy-start.2
  118.4 197.2 %all-gather.2.cloned.1.call-start = ((), (), s32[]{:S(2)}) async-start(), calls=%async_computation.1 | async-start | bytes 6635520 | tf_op jit(solution)/shard_map/all_gather | solution.py:105
Sparse Core Ops, SparseCore 0:
  118.5 196.9 all-reduce.1
Sparse Core Ops, SparseCore 1:
  120.9 81.1 all-gather.1
